TPU v7x, 32 devices: a whole 2x2x4 slice. The times are simulated.
32 devices in a mesh: row: 8 (over z, x), col: 4 (over y, core).
Axes of the slice: x: 2, y: 2, z: 4, core: 2. Of those that a mesh axis runs over, the one named last changes fastest.
Arguments:
- margin: bfloat16 [32, 128, 1152], P(('row', 'col')), may hold values from -0.2 to 1.2, as said below
- fock_matrix: bfloat16 [32, 128, 1152], P(('row', 'col')), may hold values from -0.4 to 0.4, as said below
- density: bfloat16 [32, 128, 1152], P(('row', 'col')), may hold values from -4 to 4, as said below
- present: int32 [32, 9], P(('row', 'col')), may hold values from 0 to 1, as said below
Outputs:
- gradient: float32 [32, 128, 1152], P(('row', 'col'))
- updated: float32 [32, 128, 1152], P(('row', 'col'))
Inputs may be any that keep to these rules, and one draw needn't show every extreme that they name: present[r, 4] is 1; present[r, o + 4] equals present[r + o, 4 - o]; slots whose block lies outside the matrix are 0. `margin`: symmetric: block (r, o) is the transpose of block (r + o, -o); blocks where present is 0 are zero. `fock_matrix`: symmetric: block (r, o) is the transpose of block (r + o, -o); blocks where present is 0 are zero. `density`: symmetric: block (r, o) is the transpose of block (r + o, -o); blocks where present is 0 are zero.
All inputs are finite; a program needn't handle non-finite values.
Results may differ from a plain program's by a relative error of at most 0.0041.
Values may be sent and summed in bfloat16 or wider, within the bound.
A program may use at most 64 MiB of HBM per device.

v0:
```python
import functools

import jax
import jax.numpy as jnp
from jax import lax
from jax.experimental import pallas as pl
from jax.experimental.pallas import tpu as pltpu
from jax.sharding import PartitionSpec as P

STEP_SCALE = 0.015625


def kernel(ncol, n, b, half, margin, fock, density, kept, *rest):
    outs, rest = rest[:5], rest[5:]
    (sw, xw, tw, xrow, trow, dv, fv, mv, gd, gt, gm, cf, cm, ch, co, qd, qt, base, present,
     lsem, osem, wsend, wrecv, msend, mrecv) = rest
    band = 2 * half + 1
    r = lax.axis_index("row") * ncol + lax.axis_index("col")
    k = r // 2
    core = r % 2
    chips = n // 2

    def device(t):
        return {"row": t // ncol, "col": t % ncol}

    def col(i, count=1):
        return pl.ds(pl.multiple_of(i * b, b), count * b)

    def valid_chip(e):
        return jnp.logical_and(k + e >= 0, k + e < chips)

    def valid(d):
        return jnp.logical_and(r + d >= 0, r + d < n)

    sibling = device(r + 1 - 2 * core)
    offsets = [d for d in range(-half, half + 1) if d != 0]
    reach = half // 2
    hops = [e for m in range(1, reach + 1) for e in (m, -m)]

    loads = [
        pltpu.make_async_copy(margin.at[0], mv, lsem.at[0]),
        pltpu.make_async_copy(density.at[0], dv, lsem.at[1]),
        pltpu.make_async_copy(fock.at[0], fv, lsem.at[2]),
        pltpu.make_async_copy(kept, present, lsem.at[3]),
    ]
    for c in loads:
        c.start()

    barrier = pltpu.get_barrier_semaphore()
    for d in offsets:
        @pl.when(valid(d))
        def _():
            pl.semaphore_signal(barrier, inc=1, device_id=device(r + d),
                                device_id_type=pl.DeviceIdType.MESH)

    for e in hops:
        @pl.when(jnp.logical_not(valid_chip(e)))
        def _():
            p = half + 2 * e
            for w in (sw, xw, tw):
                w[p * b:(p + 2) * b, :] = jnp.zeros((2 * b, w.shape[1]), w.dtype)
    for d in offsets:
        @pl.when(jnp.logical_not(valid(-d)))
        def _():
            for m in (gm.at[0], gm.at[1]):
                m[half - d] = jnp.zeros((b, b), gm.dtype)

    expected = jnp.minimum(r, half) + jnp.minimum(n - 1 - r, half)
    pl.semaphore_wait(barrier, expected)

    pending = []

    def window_plan(symmetric, c):
        plan = []
        for e in hops:
            m = abs(e)
            p = half - 2 * e + c
            if not symmetric:
                lo, hi = max(0, p - half), min(band, p + half)
                plan.append((e, p, lo, hi - lo + 1))
            elif e > 0:
                plan.append((e, p, 0, p + 1))
                if m == 1 and c == 1:
                    plan.append((e, p, half + 2, 2))
            else:
                plan.append((e, p, p, band + 1 - p))
                if m == 1 and c == 0:
                    plan.append((e, p, half - 2, 1))
        return plan

    def known_blocks():
        return {(p, j) for c in (0, 1) for _, p, lo, count in window_plan(True, c)
                for j in range(lo, lo + count)}

    def reflect(w, sign, own_rows):
        known = known_blocks()
        middle = (half, half + 1)
        for i in range(band + 1):
            for j in range(band + 1):
                if abs(i - j) > half or i in middle or (i, j) in known:
                    continue
                if (j in middle) != own_rows:
                    continue
                block = w[j * b:(j + 1) * b, (i + 1) * b:(i + 2) * b].T
                w[i * b:(i + 1) * b, (j + 1) * b:(j + 2) * b] = block if sign > 0 else -block

    def both(x, y):
        return jnp.logical_and(x, y)

    def spread(phase, own, w, sign, beside=None):
        here = pl.ds(pl.multiple_of((half + core) * b, b), b)
        sends, relays = [], []
        for cc in (0, 1):
            mine, theirs = core == cc, core == 1 - cc
            for i, (e, p, lo, count) in enumerate(window_plan(sign != 0, cc)):
                spot = w.at[p * b:(p + 1) * b, (lo + 1) * b:(lo + 1 + count) * b]
                s0 = lo - p + half
                send = pltpu.make_async_remote_copy(
                    src_ref=own.at[:, s0 * b:(s0 + count) * b], dst_ref=spot,
                    send_sem=wsend.at[phase, i], recv_sem=wrecv.at[phase, i],
                    device_id=device(r + 2 * e), device_id_type=pl.DeviceIdType.MESH)
                out, back = both(mine, valid_chip(e)), both(mine, valid_chip(-e))
                relay = None
                if 0 < p < band:
                    relay = pltpu.make_async_remote_copy(
                        src_ref=spot, dst_ref=spot, send_sem=wsend.at[phase, 6 + i],
                        recv_sem=wrecv.at[phase, 6 + i], device_id=sibling,
                        device_id_type=pl.DeviceIdType.MESH)
                    relays.append((relay, back, both(theirs, valid_chip(-e))))

                @pl.when(out)
                def _():
                    send.start()
                sends.append((send, relay, out, back))
        share = pltpu.make_async_remote_copy(
            src_ref=own, dst_ref=w.at[here, col(core + 1, band)],
            send_sem=wsend.at[phase, 12], recv_sem=wrecv.at[phase, 12],
            device_id=sibling, device_id_type=pl.DeviceIdType.MESH)
        share.start()
        w[here, col(core + 1, band)] = own[...]
        if sign:
            share.wait_recv()
            reflect(w, sign, True)
        if beside is not None:
            beside()
        for send, relay, out, back in sends:
            @pl.when(back)
            def _():
                send.wait_recv()
                if relay is not None:
                    relay.start()
            pending.append((out, send))
        if not sign:
            share.wait_recv()
        for relay, started, arriving in relays:
            @pl.when(arriving)
            def _():
                relay.wait_recv()
            pending.append((started, relay))
        pending.append((None, share))
        if sign:
            reflect(w, sign, False)

    def mirror(phase, left, w, own, m):
        product(left, w, own, (half,))
        copies = []
        for i, d in enumerate(sorted(offsets, key=lambda v: -abs(v))):
            product(left, w, own, (half + d,))
            c = pltpu.make_async_remote_copy(
                src_ref=own.at[:, (half + d) * b:(half + d + 1) * b],
                dst_ref=m.at[half - d], send_sem=msend.at[phase, i],
                recv_sem=mrecv.at[phase, i], device_id=device(r + d),
                device_id_type=pl.DeviceIdType.MESH)

            @pl.when(valid(d))
            def _():
                c.start()
            copies.append((d, c))
        m[half] = own[:, half * b:(half + 1) * b]
        for d, c in copies:
            @pl.when(valid(-d))
            def _():
                c.wait_recv()
            pending.append((valid(d), c))

    def product(left, w, out, columns=None):
        for c in columns or range(band):
            lo, hi = max(0, c - half), min(band, c + half + 1)
            rhs = w[pl.ds(pl.multiple_of((core + lo) * b, b), (hi - lo) * b), col(core + 1 + c)]
            acc = jnp.dot(left[:, lo * b:hi * b], rhs, preferred_element_type=jnp.float32)
            keep = present[0, c].astype(jnp.float32)
            out[:, c * b:(c + 1) * b] = (acc * keep).astype(out.dtype)

    def transposed_first():
        for c in range(band):
            lo, hi = max(0, c - half), min(band, c + half + 1)
            rhs = xw[pl.ds(pl.multiple_of((core + c) * b, b), b), col(core + 1 + lo, hi - lo)]
            acc = lax.dot_general(trow[:, lo * b:hi * b], rhs, (((1,), (1,)), ((), ())),
                                  preferred_element_type=jnp.float32)
            keep = present[0, c].astype(jnp.float32)
            cm[:, c * b:(c + 1) * b] = (acc * -keep).astype(cm.dtype)

    stores = []

    def store(src):
        i = len(stores)
        c = pltpu.make_async_copy(src, outs[i].at[0], osem.at[i])
        c.start()
        stores.append(c)

    loads[0].wait()
    spread(0, mv, sw, 1)
    loads[1].wait()
    loads[3].wait()
    product(dv, sw, xrow)
    spread(1, xrow, xw, 0)
    loads[2].wait()
    mirror(0, fv, xw, gd, gm.at[0])
    store(gd)
    for c in range(band):
        cols = slice(c * b, (c + 1) * b)
        other = gm[0, c].T
        gt[:, cols] = other
        g = gd[:, cols].astype(jnp.float32) - other.astype(jnp.float32)
        trow[:, cols] = (-STEP_SCALE * g).astype(trow.dtype)
    store(gt)
    spread(2, trow, tw, -1, transposed_first)
    product(xrow, tw, cf)
    v = cf[...].astype(jnp.float32) + cm[...].astype(jnp.float32)
    ch[...] = v.astype(ch.dtype)
    base[...] = dv[...].astype(jnp.float32) + v
    store(base)
    product(ch, sw, co)
    mirror(1, co, tw, qd, gm.at[1])
    store(qd)
    for c in range(band):
        qt[:, c * b:(c + 1) * b] = gm[1, c].T
    store(qt)
    for c in stores:
        c.wait()
    for cond, c in pending:
        if cond is None:
            c.wait_send()
        else:
            @pl.when(cond)
            def _():
                c.wait_send()


def local(ncol, n, margin, fock_matrix, density, present):
    rows, b, width = margin.shape
    band = present.shape[1]
    half = (band - 1) // 2
    bf = jnp.bfloat16
    row = pltpu.VMEM((b, width), bf)
    wide = pltpu.VMEM(((band + 1) * b, (band + 3) * b), bf)
    out = jax.ShapeDtypeStruct((rows, b, width), bf)
    outs = pl.pallas_call(
        functools.partial(kernel, ncol, n, b, half),
        out_shape=(out, out, jax.ShapeDtypeStruct((rows, b, width), jnp.float32), out, out),
        in_specs=[pl.BlockSpec(memory_space=pltpu.HBM)] * 4,
        out_specs=[pl.BlockSpec(memory_space=pltpu.HBM)] * 5,
        scratch_shapes=[
            wide, wide, wide, row, row, row, row, row,
            row, row, pltpu.VMEM((2, band, b, b), bf), row, row, row, row, row, row,
            pltpu.VMEM((b, width), jnp.float32), pltpu.SMEM((rows, band), jnp.int32),
            pltpu.SemaphoreType.DMA((4,)),
            pltpu.SemaphoreType.DMA((5,)),
            pltpu.SemaphoreType.DMA((3, 13)),
            pltpu.SemaphoreType.DMA((3, 13)),
            pltpu.SemaphoreType.DMA((2, 2 * half)),
            pltpu.SemaphoreType.DMA((2, 2 * half)),
        ],
        compiler_params=pltpu.CompilerParams(
            collective_id=0, has_side_effects=True, vmem_limit_bytes=67043328),
        name="density_step",
    )(margin, fock_matrix, density, present)
    gd, gt, base, qd, qt = (v.astype(jnp.float32) for v in outs)
    return gd - gt, base + 0.5 * (qd + qt)


def solution(mesh):
    nrow, ncol = mesh.shape["row"], mesh.shape["col"]
    spec3 = P(("row", "col"), None, None)
    return jax.shard_map(
        functools.partial(local, ncol, nrow * ncol), mesh=mesh,
        in_specs=(spec3, spec3, spec3, P(("row", "col"), None)),
        out_specs=(spec3, spec3), check_vma=False)
```

profile of v0, /device:TPU:17, one launch (start us, length us, event | category | flops | bytes accessed | tf_op | source)
XLA Modules:
  0.0 54.9 jit_solution(9798300085798066787)
XLA Ops:
  0.6 51.7 %density_step.1 = (bf16[1,128,1152]{2,1,0:T(8,128)(2,1)}, bf16[1,128,1152]{2,1,0:T(8,128)(2,1)}, f32[1,128,1152]{2,1,0:T(8,128)}, bf16[1,128,1152]{2,1,0:T(8,128)(2,1)}, bf16[1,128,1152]{2,1,0:T(8,128)(2,1)}) custom-call(bf16[1,128,1152]{2,1,0:T(8,128)(2,1)} %margin.1, bf16[1,128,1152]{2,1,0:T(8,128)(2,1)} %fock.1, bf16[1,128,1152]{2,1,0:T(8,128)(2,1)} %density.1, ...), custom_call_target="tpu_custom_call" | custom-call | tf_op jit(solution)/shard_map/density_step/pallas_call | solution.py:258
  52.4 2.6 %multiply_add_fusion = (f32[1,128,1152]{2,1,0:T(8,128)}, f32[1,128,1152]{2,1,0:T(8,128)}) fusion(f32[1,128,1152]{2,1,0:T(8,128)} %get-tuple-element.9, bf16[1,128,1152]{2,1,0:T(8,128)(2,1)} %get-tuple-element.11, bf16[1,128,1152]{2,1,0:T(8,128)(2,1)} %get-tuple-element.10, bf16[1,128,1152]{2,1,0:T(8,128)(2,1)} %get-tuple-element.8, ...), kind=kLoop, calls=%fused_computation | loop fusion | flops 1179648 | bytes 2949120 | tf_op jit(solution)/shard_map/add | solution.py:279
where the time goes:
time: 55.3 us; the launch traced here: 54.9 us
  Pallas kernels  51.7 us (93%)
  other arithmetic  2.57 us (5%)
  between operations  0.64 us (1%)
    pallas_call x1, Pallas kernels, local(): pl.pallas_call(functools.partial(kernel, ncol, n, b, half), out_shape=(ou...  51.7 us
    add x1, other arithmetic, local(): return (gd - gt, base + 0.5 * (qd + qt))  2.57 us

commit v1 on v0

v1 whole, which is shorter than its diff:
```python
import functools

import jax
import jax.numpy as jnp
from jax import lax
from jax.experimental import pallas as pl
from jax.experimental.pallas import tpu as pltpu
from jax.sharding import PartitionSpec as P

STEP_SCALE = 0.015625


def runs(columns):
    out = []
    for j in sorted(columns):
        if out and out[-1][0] + out[-1][1] == j:
            out[-1] = (out[-1][0], out[-1][1] + 1)
        else:
            out.append((j, 1))
    return out


def receive_plan(half, parity):
    band = 2 * half + 1
    own = (half, half + 1)
    partner = 1 - 2 * parity
    owned = {}
    for i in range(band + 1):
        for j in range(i, band + 1):
            if j - i > half or i in own or j in own:
                continue
            chips = {i // 2 - half // 2, j // 2 - half // 2}
            rank = lambda e: (e != partner, e % 2 != 0, abs(e))
            owned.setdefault(min(chips, key=rank), []).append((i, j))
    plan = {}
    for e, pairs in owned.items():
        low = 2 * e + half
        options = []
        for pick in (0, 1):
            rows = {low: set(), low + 1: set()}
            for i, j in pairs:
                if i in rows and j in rows:
                    row = (i, j)[pick]
                    rows[row].add(i + j - row)
                elif i in rows:
                    rows[i].add(j)
                else:
                    rows[j].add(i)
            options.append({p: runs(c) for p, c in rows.items()})
        best = min(options, key=lambda o: sum(len(v) for v in o.values()))
        for p, v in best.items():
            plan[e, p] = v
    return plan


def kernel(ncol, n, b, half, margin, fock, density, kept, *rest):
    outs, rest = rest[:5], rest[5:]
    (dw, fw, sw, tw, zrow, xrow, trow, dv, fv, mv, gd, gt, gm, cf, ch, co, qd, qt, base, present,
     lsem, osem, wsend, wrecv, msend, mrecv) = rest
    band = 2 * half + 1
    r = lax.axis_index("row") * ncol + lax.axis_index("col")
    k = r // 2
    core = r % 2
    chips = n // 2
    parity = k % 2

    def device(t):
        return {"row": t // ncol, "col": t % ncol}

    def col(i, count=1):
        return pl.ds(pl.multiple_of(i * b, b), count * b)

    def valid_chip(e):
        return jnp.logical_and(k + e >= 0, k + e < chips)

    def valid(d):
        return jnp.logical_and(r + d >= 0, r + d < n)

    def both(x, y):
        return jnp.logical_and(x, y)

    sibling = device(r + 1 - 2 * core)
    offsets = [d for d in range(-half, half + 1) if d != 0]
    reach = half // 2
    hops = [e for m in range(reach, 0, -1) for e in (m, -m)]
    received = [receive_plan(half, q) for q in (0, 1)]

    loads = [
        pltpu.make_async_copy(density.at[0], dv, lsem.at[0]),
        pltpu.make_async_copy(fock.at[0], fv, lsem.at[1]),
        pltpu.make_async_copy(margin.at[0], mv, lsem.at[2]),
        pltpu.make_async_copy(kept, present, lsem.at[3]),
    ]
    for c in loads:
        c.start()

    barrier = pltpu.get_barrier_semaphore()
    for d in offsets:
        @pl.when(valid(d))
        def _():
            pl.semaphore_signal(barrier, inc=1, device_id=device(r + d),
                                device_id_type=pl.DeviceIdType.MESH)

    for e in hops:
        @pl.when(jnp.logical_not(valid_chip(e)))
        def _():
            p = half + 2 * e
            for w in (dw, fw, sw, tw):
                w[p * b:(p + 2) * b, :] = jnp.zeros((2 * b, w.shape[1]), w.dtype)
    for d in offsets:
        @pl.when(jnp.logical_not(valid(-d)))
        def _():
            for m in range(gm.shape[0]):
                gm[m, half - d] = jnp.zeros((b, b), gm.dtype)

    expected = jnp.minimum(r, half) + jnp.minimum(n - 1 - r, half)
    pl.semaphore_wait(barrier, expected)

    pending = []

    def reflect(w, sign, own_rows):
        middle = (half, half + 1)
        for q in (0, 1):
            known = {(p, j) for (_, p), v in received[q].items() for lo, count in v
                     for j in range(lo, lo + count)}
            todo = [(i, j) for i in range(band + 1) for j in range(band + 1)
                    if abs(i - j) <= half and i not in middle and (i, j) not in known
                    and (j in middle) == own_rows]

            def fill(todo=todo):
                for i, j in todo:
                    block = w[j * b:(j + 1) * b, (i + 1) * b:(i + 2) * b].T
                    w[i * b:(i + 1) * b, (j + 1) * b:(j + 2) * b] = block if sign > 0 else -block

            if own_rows:
                fill()
                return
            pl.when(parity == q)(fill)

    def spread_start(phase, own, w):
        here = pl.ds(pl.multiple_of((half + core) * b, b), b)
        share = pltpu.make_async_remote_copy(
            src_ref=own, dst_ref=w.at[here, col(core + 1, band)],
            send_sem=wsend.at[phase, 0], recv_sem=wrecv.at[phase, 0],
            device_id=sibling, device_id_type=pl.DeviceIdType.MESH)
        sends, relays = [], []
        for a, e in enumerate(hops):
            for q in (0, 1):
                for cc in (0, 1):
                    p = half - 2 * e + cc
                    for u, (lo, count) in enumerate(received[q].get((-e, p), [])):
                        slot = 1 + 2 * a + u
                        spot = w.at[p * b:(p + 1) * b, (lo + 1) * b:(lo + 1 + count) * b]
                        s0 = lo - p + half
                        send = pltpu.make_async_remote_copy(
                            src_ref=own.at[:, s0 * b:(s0 + count) * b], dst_ref=spot,
                            send_sem=wsend.at[phase, slot], recv_sem=wrecv.at[phase, slot],
                            device_id=device(r + 2 * e), device_id_type=pl.DeviceIdType.MESH)
                        relay = pltpu.make_async_remote_copy(
                            src_ref=spot, dst_ref=spot, send_sem=wsend.at[phase, 8 + slot],
                            recv_sem=wrecv.at[phase, 8 + slot], device_id=sibling,
                            device_id_type=pl.DeviceIdType.MESH)
                        out = both(both(core == cc, parity == (q + e) % 2), valid_chip(e))
                        back = both(both(core == cc, parity == q), valid_chip(-e))
                        theirs = both(both(core == 1 - cc, parity == q), valid_chip(-e))

                        @pl.when(out)
                        def _():
                            send.start()
                        sends.append((send, relay, out, back))
                        relays.append((relay, back, theirs))
        share.start()
        w[here, col(core + 1, band)] = own[...]
        return share, sends, relays

    def spread_finish(w, sign, flight, beside=None):
        share, sends, relays = flight
        share.wait_recv()
        reflect(w, sign, True)
        if beside is not None:
            beside()
        for send, relay, out, back in reversed(sends):
            @pl.when(back)
            def _():
                send.wait_recv()
                relay.start()
            pending.append((out, send))
        for relay, started, arriving in reversed(relays):
            @pl.when(arriving)
            def _():
                relay.wait_recv()
            pending.append((started, relay))
        pending.append((None, share))
        reflect(w, sign, False)

    def mirror(phase, left, w, own, m):
        copies = []
        for i, d in enumerate(sorted(offsets, key=lambda v: -abs(v))):
            product(left, w, own, (half + d,))
            c = pltpu.make_async_remote_copy(
                src_ref=own.at[:, (half + d) * b:(half + d + 1) * b],
                dst_ref=m.at[half - d], send_sem=msend.at[phase, i],
                recv_sem=mrecv.at[phase, i], device_id=device(r + d),
                device_id_type=pl.DeviceIdType.MESH)

            @pl.when(valid(d))
            def _():
                c.start()
            copies.append((d, c))
        product(left, w, own, (half,))
        m[half] = own[:, half * b:(half + 1) * b]
        for d, c in copies:
            pending.append((valid(d), c))
        return copies

    def mirror_wait(copies):
        for d, c in copies:
            @pl.when(valid(-d))
            def _():
                c.wait_recv()

    def product(left, w, out, columns=None):
        for c in columns or range(band):
            lo, hi = max(0, c - half), min(band, c + half + 1)
            rhs = w[pl.ds(pl.multiple_of((core + lo) * b, b), (hi - lo) * b), col(core + 1 + c)]
            acc = jnp.dot(left[:, lo * b:hi * b], rhs, preferred_element_type=jnp.float32)
            keep = present[0, c].astype(jnp.float32)
            out[:, c * b:(c + 1) * b] = (acc * keep).astype(out.dtype)

    stores = []

    def store(src):
        i = len(stores)
        c = pltpu.make_async_copy(src, outs[i].at[0], osem.at[i])
        c.start()
        stores.append(c)

    def body():
        loads[0].wait()
        dflight = spread_start(0, dv, dw)
        loads[1].wait()
        fflight = spread_start(1, fv, fw)
        loads[2].wait()
        loads[3].wait()
        sflight = spread_start(2, mv, sw)
        spread_finish(dw, 1, dflight)
        product(mv, dw, zrow)
        spread_finish(fw, 1, fflight)
        copies = mirror(0, zrow, fw, gd, gm.at[0])
        store(gd)
        mirror_wait(copies)
        for c in range(band):
            cols = slice(c * b, (c + 1) * b)
            other = gm[0, c].T
            gt[:, cols] = other
            g = other.astype(jnp.float32) - gd[:, cols].astype(jnp.float32)
            trow[:, cols] = (-STEP_SCALE * g).astype(trow.dtype)
        store(gt)
        tflight = spread_start(3, trow, tw)

        def beside():
            spread_finish(sw, 1, sflight)
            product(dv, sw, xrow)

        spread_finish(tw, -1, tflight, beside)
        copies = mirror(1, xrow, tw, cf, gm.at[1])
        mirror_wait(copies)
        for c in range(band):
            cols = slice(c * b, (c + 1) * b)
            v = cf[:, cols].astype(jnp.float32) + gm[1, c].T.astype(jnp.float32)
            ch[:, cols] = v.astype(ch.dtype)
            base[:, cols] = dv[:, cols].astype(jnp.float32) + v
        store(base)
        product(ch, sw, co)
        copies = mirror(2, co, tw, qd, gm.at[2])
        store(qd)
        mirror_wait(copies)
        for c in range(band):
            qt[:, c * b:(c + 1) * b] = gm[2, c].T
        store(qt)

    body()
    for c in stores:
        c.wait()
    for cond, c in pending:
        if cond is None:
            c.wait_send()
        else:
            @pl.when(cond)
            def _():
                c.wait_send()


def local(ncol, n, margin, fock_matrix, density, present):
    rows, b, width = margin.shape
    band = present.shape[1]
    half = (band - 1) // 2
    bf = jnp.bfloat16
    row = pltpu.VMEM((b, width), bf)
    wide = pltpu.VMEM(((band + 1) * b, (band + 3) * b), bf)
    out = jax.ShapeDtypeStruct((rows, b, width), bf)
    outs = pl.pallas_call(
        functools.partial(kernel, ncol, n, b, half),
        out_shape=(out, out, jax.ShapeDtypeStruct((rows, b, width), jnp.float32), out, out),
        in_specs=[pl.BlockSpec(memory_space=pltpu.HBM)] * 4,
        out_specs=[pl.BlockSpec(memory_space=pltpu.HBM)] * 5,
        scratch_shapes=[
            wide, wide, wide, wide, row, row, row, row, row, row,
            row, row, pltpu.VMEM((3, band, b, b), bf), row, row, row, row, row,
            pltpu.VMEM((b, width), jnp.float32), pltpu.SMEM((rows, band), jnp.int32),
            pltpu.SemaphoreType.DMA((4,)),
            pltpu.SemaphoreType.DMA((5,)),
            pltpu.SemaphoreType.DMA((4, 17)),
            pltpu.SemaphoreType.DMA((4, 17)),
            pltpu.SemaphoreType.DMA((3, 2 * half)),
            pltpu.SemaphoreType.DMA((3, 2 * half)),
        ],
        compiler_params=pltpu.CompilerParams(
            collective_id=0, has_side_effects=True, vmem_limit_bytes=67043328),
        name="density_step",
    )(margin, fock_matrix, density, present)
    gd, gt, base, qd, qt = (v.astype(jnp.float32) for v in outs)
    return gt - gd, base + 0.5 * (qd + qt)


def solution(mesh):
    nrow, ncol = mesh.shape["row"], mesh.shape["col"]
    spec3 = P(("row", "col"), None, None)
    return jax.shard_map(
        functools.partial(local, ncol, nrow * ncol), mesh=mesh,
        in_specs=(spec3, spec3, spec3, P(("row", "col"), None)),
        out_specs=(spec3, spec3), check_vma=False)
```

time: 55.3 us -> 51.6 us (0.933)
  Pallas kernels: 51.7 us -> 47.8 us
    pallas_call x1, Pallas kernels: 51.7 us -> 47.8 us  [local(): pl.pallas_call(functools.partial(kernel, ncol, n, b, half), out_shape=(ou...]
where the time goes in v1:
time: 51.6 us; the launch traced here: 51 us
  Pallas kernels  47.8 us (93%)
  other arithmetic  2.57 us (5%)
  between operations  0.64 us (1%)
    pallas_call x1, Pallas kernels, local(): pl.pallas_call(functools.partial(kernel, ncol, n, b, half), out_shape=(ou...  47.8 us
    add x1, other arithmetic, local(): return (gt - gd, base + 0.5 * (qd + qt))  2.57 us

profile of v1, /device:TPU:17, one launch (start us, length us, event | category | flops | bytes accessed | tf_op | source)
XLA Modules:
  0.0 51.0 jit_solution(2319708125632358470)
XLA Ops:
  0.6 47.8 %density_step.1 = (bf16[1,128,1152]{2,1,0:T(8,128)(2,1)}, bf16[1,128,1152]{2,1,0:T(8,128)(2,1)}, f32[1,128,1152]{2,1,0:T(8,128)}, bf16[1,128,1152]{2,1,0:T(8,128)(2,1)}, bf16[1,128,1152]{2,1,0:T(8,128)(2,1)}) custom-call(bf16[1,128,1152]{2,1,0:T(8,128)(2,1)} %margin.1, bf16[1,128,1152]{2,1,0:T(8,128)(2,1)} %fock.1, bf16[1,128,1152]{2,1,0:T(8,128)(2,1)} %density.1, ...), custom_call_target="tpu_custom_call" | custom-call | tf_op jit(solution)/shard_map/density_step/pallas_call | solution.py:302
  48.5 2.6 %multiply_add_fusion = (f32[1,128,1152]{2,1,0:T(8,128)}, f32[1,128,1152]{2,1,0:T(8,128)}) fusion(f32[1,128,1152]{2,1,0:T(8,128)} %get-tuple-element.9, bf16[1,128,1152]{2,1,0:T(8,128)(2,1)} %get-tuple-element.11, bf16[1,128,1152]{2,1,0:T(8,128)(2,1)} %get-tuple-element.10, bf16[1,128,1152]{2,1,0:T(8,128)(2,1)} %get-tuple-element.8, ...), kind=kLoop, calls=%fused_computation | loop fusion | flops 1179648 | bytes 2949120 | tf_op jit(solution)/shard_map/add | solution.py:323

commit v2 on v1

--- a/solution.py
+++ b/solution.py
@@ -55,8 +55,9 @@
 
 def kernel(ncol, n, b, half, margin, fock, density, kept, *rest):
     outs, rest = rest[:5], rest[5:]
-    (dw, fw, sw, tw, zrow, xrow, trow, dv, fv, mv, gd, gt, gm, cf, ch, co, qd, qt, base, present,
-     lsem, osem, wsend, wrecv, msend, mrecv) = rest
+    gd, gt, base, qd, qt = (o.at[0] for o in outs)
+    (dw, fw, sw, tw, zrow, xrow, trow, dv, fv, mv, gm, cf, ch, co, present,
+     lsem, wsend, wrecv, msend, mrecv) = rest
     band = 2 * half + 1
     r = lax.axis_index("row") * ncol + lax.axis_index("col")
     k = r // 2
@@ -84,6 +85,8 @@
     reach = half // 2
     hops = [e for m in range(reach, 0, -1) for e in (m, -m)]
     received = [receive_plan(half, q) for q in (0, 1)]
+    near = 2
+    spots = len(hops) + near
 
     loads = [
         pltpu.make_async_copy(density.at[0], dv, lsem.at[0]),
@@ -118,6 +121,14 @@
 
     pending = []
 
+    def drain():
+        for cond, c in pending:
+            if cond is None:
+                c.wait_send()
+            else:
+                pl.when(cond)(c.wait_send)
+        pending.clear()
+
     def reflect(w, sign, own_rows):
         middle = (half, half + 1)
         for q in (0, 1):
@@ -137,7 +148,7 @@
                 return
             pl.when(parity == q)(fill)
 
-    def spread_start(phase, own, w):
+    def spread_plan(phase, own, w):
         here = pl.ds(pl.multiple_of((half + core) * b, b), b)
         share = pltpu.make_async_remote_copy(
             src_ref=own, dst_ref=w.at[here, col(core + 1, band)],
@@ -149,7 +160,7 @@
                 for cc in (0, 1):
                     p = half - 2 * e + cc
                     for u, (lo, count) in enumerate(received[q].get((-e, p), [])):
-                        slot = 1 + 2 * a + u
+                        slot = 1 + a + (len(hops) - near) * u
                         spot = w.at[p * b:(p + 1) * b, (lo + 1) * b:(lo + 1 + count) * b]
                         s0 = lo - p + half
                         send = pltpu.make_async_remote_copy(
@@ -157,28 +168,28 @@
                             send_sem=wsend.at[phase, slot], recv_sem=wrecv.at[phase, slot],
                             device_id=device(r + 2 * e), device_id_type=pl.DeviceIdType.MESH)
                         relay = pltpu.make_async_remote_copy(
-                            src_ref=spot, dst_ref=spot, send_sem=wsend.at[phase, 8 + slot],
-                            recv_sem=wrecv.at[phase, 8 + slot], device_id=sibling,
+                            src_ref=spot, dst_ref=spot, send_sem=wsend.at[phase, spots + slot],
+                            recv_sem=wrecv.at[phase, spots + slot], device_id=sibling,
                             device_id_type=pl.DeviceIdType.MESH)
                         out = both(both(core == cc, parity == (q + e) % 2), valid_chip(e))
                         back = both(both(core == cc, parity == q), valid_chip(-e))
                         theirs = both(both(core == 1 - cc, parity == q), valid_chip(-e))
-
-                        @pl.when(out)
-                        def _():
-                            send.start()
                         sends.append((send, relay, out, back))
                         relays.append((relay, back, theirs))
+        return share, sends, relays
+
+    def spread_start(flight, w, own):
+        share, sends, _ = flight
+        here = pl.ds(pl.multiple_of((half + core) * b, b), b)
+        for send, _, out, _ in sends:
+            pl.when(out)(send.start)
         share.start()
         w[here, col(core + 1, band)] = own[...]
-        return share, sends, relays
-
-    def spread_finish(w, sign, flight, beside=None):
+
+    def spread_finish(w, sign, flight):
         share, sends, relays = flight
         share.wait_recv()
         reflect(w, sign, True)
-        if beside is not None:
-            beside()
         for send, relay, out, back in reversed(sends):
             @pl.when(back)
             def _():
@@ -227,68 +238,49 @@
             keep = present[0, c].astype(jnp.float32)
             out[:, c * b:(c + 1) * b] = (acc * keep).astype(out.dtype)
 
-    stores = []
-
-    def store(src):
-        i = len(stores)
-        c = pltpu.make_async_copy(src, outs[i].at[0], osem.at[i])
-        c.start()
-        stores.append(c)
-
     def body():
+        dflight, fflight = spread_plan(0, dv, dw), spread_plan(1, fv, fw)
+        sflight, tflight = spread_plan(2, mv, sw), spread_plan(0, trow, tw)
         loads[0].wait()
-        dflight = spread_start(0, dv, dw)
+        spread_start(dflight, dw, dv)
         loads[1].wait()
-        fflight = spread_start(1, fv, fw)
+        spread_start(fflight, fw, fv)
         loads[2].wait()
         loads[3].wait()
-        sflight = spread_start(2, mv, sw)
+        spread_start(sflight, sw, mv)
         spread_finish(dw, 1, dflight)
         product(mv, dw, zrow)
         spread_finish(fw, 1, fflight)
         copies = mirror(0, zrow, fw, gd, gm.at[0])
-        store(gd)
+        spread_finish(sw, 1, sflight)
+        product(dv, sw, xrow)
         mirror_wait(copies)
+        drain()
         for c in range(band):
             cols = slice(c * b, (c + 1) * b)
             other = gm[0, c].T
             gt[:, cols] = other
             g = other.astype(jnp.float32) - gd[:, cols].astype(jnp.float32)
             trow[:, cols] = (-STEP_SCALE * g).astype(trow.dtype)
-        store(gt)
-        tflight = spread_start(3, trow, tw)
-
-        def beside():
-            spread_finish(sw, 1, sflight)
-            product(dv, sw, xrow)
-
-        spread_finish(tw, -1, tflight, beside)
+        spread_start(tflight, tw, trow)
+
+        spread_finish(tw, -1, tflight)
         copies = mirror(1, xrow, tw, cf, gm.at[1])
         mirror_wait(copies)
+        drain()
         for c in range(band):
             cols = slice(c * b, (c + 1) * b)
             v = cf[:, cols].astype(jnp.float32) + gm[1, c].T.astype(jnp.float32)
             ch[:, cols] = v.astype(ch.dtype)
             base[:, cols] = dv[:, cols].astype(jnp.float32) + v
-        store(base)
         product(ch, sw, co)
-        copies = mirror(2, co, tw, qd, gm.at[2])
-        store(qd)
+        copies = mirror(0, co, tw, qd, gm.at[2])
         mirror_wait(copies)
         for c in range(band):
             qt[:, c * b:(c + 1) * b] = gm[2, c].T
-        store(qt)
 
     body()
-    for c in stores:
-        c.wait()
-    for cond, c in pending:
-        if cond is None:
-            c.wait_send()
-        else:
-            @pl.when(cond)
-            def _():
-                c.wait_send()
+    drain()
 
 
 def local(ncol, n, margin, fock_matrix, density, present):
@@ -303,22 +295,20 @@
         functools.partial(kernel, ncol, n, b, half),
         out_shape=(out, out, jax.ShapeDtypeStruct((rows, b, width), jnp.float32), out, out),
         in_specs=[pl.BlockSpec(memory_space=pltpu.HBM)] * 4,
-        out_specs=[pl.BlockSpec(memory_space=pltpu.HBM)] * 5,
+        out_specs=[pl.BlockSpec(memory_space=pltpu.VMEM)] * 5,
         scratch_shapes=[
             wide, wide, wide, wide, row, row, row, row, row, row,
-            row, row, pltpu.VMEM((3, band, b, b), bf), row, row, row, row, row,
-            pltpu.VMEM((b, width), jnp.float32), pltpu.SMEM((rows, band), jnp.int32),
+            pltpu.VMEM((3, band, b, b), bf), row, row, row, pltpu.SMEM((rows, band), jnp.int32),
             pltpu.SemaphoreType.DMA((4,)),
-            pltpu.SemaphoreType.DMA((5,)),
-            pltpu.SemaphoreType.DMA((4, 17)),
-            pltpu.SemaphoreType.DMA((4, 17)),
-            pltpu.SemaphoreType.DMA((3, 2 * half)),
-            pltpu.SemaphoreType.DMA((3, 2 * half)),
+            pltpu.SemaphoreType.DMA((3, 5 + 2 * half)),
+            pltpu.SemaphoreType.DMA((3, 5 + 2 * half)),
+            pltpu.SemaphoreType.DMA((2, 2 * half)),
+            pltpu.SemaphoreType.DMA((2, 2 * half)),
         ],
         compiler_params=pltpu.CompilerParams(
-            collective_id=0, has_side_effects=True, vmem_limit_bytes=67043328),
+            collective_id=0, has_side_effects=True, vmem_limit_bytes=30000000),
         name="density_step",
-    )(margin, fock_matrix, density, present)
+    )(*(pltpu.with_memory_space_constraint(v, pltpu.HBM) for v in (margin, fock_matrix, density, present)))
     gd, gt, base, qd, qt = (v.astype(jnp.float32) for v in outs)
     return gt - gd, base + 0.5 * (qd + qt)
 

time: 51.6 us -> 48 us (0.930)
  Pallas kernels: 47.8 us -> 46.1 us
  other arithmetic: 2.57 us -> 1.17 us
    pallas_call x1, Pallas kernels: 47.8 us -> 46.1 us  [local(): pl.pallas_call(functools.partial(kernel, ncol, n, b, half), out_shape=(ou...]
    add x1, other arithmetic: 2.57 us -> 1.17 us  [local(): return (gt - gd, base + 0.5 * (qd + qt))]
where the time goes in v2:
time: 48 us; the launch traced here: 47.9 us
  Pallas kernels  46.1 us (96%)
  other arithmetic  1.17 us (2%)
  between operations  0.64 us (1%)
    pallas_call x1, Pallas kernels, local(): pl.pallas_call(functools.partial(kernel, ncol, n, b, half), out_shape=(ou...  46.1 us
    add x1, other arithmetic, local(): return (gt - gd, base + 0.5 * (qd + qt))  1.17 us

profile of v2, /device:TPU:17, one launch (start us, length us, event | category | flops | bytes accessed | tf_op | source)
XLA Modules:
  0.0 47.9 jit_solution(445252640457992423)
XLA Ops:
  0.6 46.1 %density_step.1 = (bf16[1,128,1152]{2,1,0:T(8,128)(2,1)S(1)}, bf16[1,128,1152]{2,1,0:T(8,128)(2,1)S(1)}, f32[1,128,1152]{2,1,0:T(8,128)S(1)}, bf16[1,128,1152]{2,1,0:T(8,128)(2,1)S(1)}, bf16[1,128,1152]{2,1,0:T(8,128)(2,1)S(1)}) custom-call(bf16[1,128,1152]{2,1,0:T(8,128)(2,1)} %margin.1, bf16[1,128,1152]{2,1,0:T(8,128)(2,1)} %fock.1, ...), custom_call_target="tpu_custom_call" | custom-call | tf_op jit(solution)/shard_map/density_step/pallas_call | solution.py:294
  46.7 1.2 %multiply_add_fusion = (f32[1,128,1152]{2,1,0:T(8,128)}, f32[1,128,1152]{2,1,0:T(8,128)}) fusion(f32[1,128,1152]{2,1,0:T(8,128)S(1)} %get-tuple-element.9, bf16[1,128,1152]{2,1,0:T(8,128)(2,1)S(1)} %get-tuple-element.11, bf16[1,128,1152]{2,1,0:T(8,128)(2,1)S(1)} %get-tuple-element.10, bf16[1,128,1152]{2,1,0:T(8,128)(2,1)S(1)} %get-tuple-element.8, ...), kind=kLoop, calls=%fused_computation | loop fusion | flops 1179648 | bytes 2949120 | tf_op jit(solution)/shard_map/add | solution.py:313

commit v3 on v2

--- a/solution.py
+++ b/solution.py
@@ -84,6 +84,7 @@
     offsets = [d for d in range(-half, half + 1) if d != 0]
     reach = half // 2
     hops = [e for m in range(reach, 0, -1) for e in (m, -m)]
+    send_order = sorted(hops, key=abs)
     received = [receive_plan(half, q) for q in (0, 1)]
     near = 2
     spots = len(hops) + near
@@ -121,13 +122,7 @@
 
     pending = []
 
-    def drain():
-        for cond, c in pending:
-            if cond is None:
-                c.wait_send()
-            else:
-                pl.when(cond)(c.wait_send)
-        pending.clear()
+    flights = []
 
     def reflect(w, sign, own_rows):
         middle = (half, half + 1)
@@ -154,7 +149,7 @@
             src_ref=own, dst_ref=w.at[here, col(core + 1, band)],
             send_sem=wsend.at[phase, 0], recv_sem=wrecv.at[phase, 0],
             device_id=sibling, device_id_type=pl.DeviceIdType.MESH)
-        sends, relays = [], []
+        moves = []
         for a, e in enumerate(hops):
             for q in (0, 1):
                 for cc in (0, 1):
@@ -171,38 +166,75 @@
                             src_ref=spot, dst_ref=spot, send_sem=wsend.at[phase, spots + slot],
                             recv_sem=wrecv.at[phase, spots + slot], device_id=sibling,
                             device_id_type=pl.DeviceIdType.MESH)
-                        out = both(both(core == cc, parity == (q + e) % 2), valid_chip(e))
-                        back = both(both(core == cc, parity == q), valid_chip(-e))
-                        theirs = both(both(core == 1 - cc, parity == q), valid_chip(-e))
-                        sends.append((send, relay, out, back))
-                        relays.append((relay, back, theirs))
-        return share, sends, relays
-
-    def spread_start(flight, w, own):
-        share, sends, _ = flight
+                        moves.append((send, relay, e, q, cc, -e == 1 - 2 * q))
+        return share, moves
+
+    def spread_start(flight):
+        for z in (0, 1):
+            for cc in (0, 1):
+                @pl.when(both(parity == z, core == cc))
+                def _():
+                    for send, _, e, q, c, partner in sorted(flight[1], key=lambda m: send_order.index(m[2])):
+                        if (q + e) % 2 == z and c == cc:
+                            if partner:
+                                send.start()
+                            else:
+                                pl.when(valid_chip(e))(send.start)
+
+    def spread_share(flight, w, own):
         here = pl.ds(pl.multiple_of((half + core) * b, b), b)
-        for send, _, out, _ in sends:
-            pl.when(out)(send.start)
-        share.start()
+        flight[0].start()
         w[here, col(core + 1, band)] = own[...]
 
     def spread_finish(w, sign, flight):
-        share, sends, relays = flight
+        share, moves = flight
         share.wait_recv()
         reflect(w, sign, True)
-        for send, relay, out, back in reversed(sends):
-            @pl.when(back)
-            def _():
-                send.wait_recv()
-                relay.start()
-            pending.append((out, send))
-        for relay, started, arriving in reversed(relays):
-            @pl.when(arriving)
-            def _():
-                relay.wait_recv()
-            pending.append((started, relay))
-        pending.append((None, share))
+        ordered = sorted(moves, key=lambda m: (not m[5], -abs(m[2])))
+        for z in (0, 1):
+            for cc in (0, 1):
+                @pl.when(both(parity == z, core == cc))
+                def _():
+                    for send, relay, e, q, c, partner in ordered:
+                        if q == z and c == cc:
+                            def arrive():
+                                send.wait_recv()
+                                relay.start()
+                            if partner:
+                                arrive()
+                            else:
+                                pl.when(valid_chip(-e))(arrive)
+                    for send, relay, e, q, c, partner in ordered:
+                        if q == z and c == 1 - cc:
+                            if partner:
+                                relay.wait_recv()
+                            else:
+                                pl.when(valid_chip(-e))(relay.wait_recv)
+        flights.append(flight)
         reflect(w, sign, False)
+
+    def drain():
+        for share, moves in flights:
+            share.wait_send()
+            for z in (0, 1):
+                for cc in (0, 1):
+                    @pl.when(both(parity == z, core == cc))
+                    def _():
+                        for send, relay, e, q, c, partner in moves:
+                            if (q + e) % 2 == z and c == cc:
+                                if partner:
+                                    send.wait_send()
+                                else:
+                                    pl.when(valid_chip(e))(send.wait_send)
+                            if q == z and c == cc:
+                                if partner:
+                                    relay.wait_send()
+                                else:
+                                    pl.when(valid_chip(-e))(relay.wait_send)
+        flights.clear()
+        for cond, c in pending:
+            pl.when(cond)(c.wait_send)
+        pending.clear()
 
     def mirror(phase, left, w, own, m):
         copies = []
@@ -224,11 +256,11 @@
             pending.append((valid(d), c))
         return copies
 
-    def mirror_wait(copies):
+    def mirror_use(copies, use):
         for d, c in copies:
-            @pl.when(valid(-d))
-            def _():
-                c.wait_recv()
+            pl.when(valid(-d))(c.wait_recv)
+        for o in range(-half, half + 1):
+            use(o)
 
     def product(left, w, out, columns=None):
         for c in columns or range(band):
@@ -238,46 +270,53 @@
             keep = present[0, c].astype(jnp.float32)
             out[:, c * b:(c + 1) * b] = (acc * keep).astype(out.dtype)
 
+    def columns(o):
+        return slice((half + o) * b, (half + o + 1) * b)
+
+    def gradient(o):
+        other = gm[0, half + o].T
+        gt[:, columns(o)] = other
+        g = other.astype(jnp.float32) - gd[:, columns(o)].astype(jnp.float32)
+        trow[:, columns(o)] = (-STEP_SCALE * g).astype(trow.dtype)
+
+    def commute(o):
+        v = cf[:, columns(o)].astype(jnp.float32) + gm[1, half + o].T.astype(jnp.float32)
+        ch[:, columns(o)] = v.astype(ch.dtype)
+        base[:, columns(o)] = dv[:, columns(o)].astype(jnp.float32) + v
+
+    def second(o):
+        qt[:, columns(o)] = gm[2, half + o].T
+
     def body():
         dflight, fflight = spread_plan(0, dv, dw), spread_plan(1, fv, fw)
         sflight, tflight = spread_plan(2, mv, sw), spread_plan(0, trow, tw)
         loads[0].wait()
-        spread_start(dflight, dw, dv)
+        spread_start(dflight)
+        spread_share(dflight, dw, dv)
         loads[1].wait()
-        spread_start(fflight, fw, fv)
+        spread_start(fflight)
+        spread_share(fflight, fw, fv)
         loads[2].wait()
         loads[3].wait()
-        spread_start(sflight, sw, mv)
         spread_finish(dw, 1, dflight)
+        spread_start(sflight)
+        spread_share(sflight, sw, mv)
         product(mv, dw, zrow)
         spread_finish(fw, 1, fflight)
         copies = mirror(0, zrow, fw, gd, gm.at[0])
         spread_finish(sw, 1, sflight)
         product(dv, sw, xrow)
-        mirror_wait(copies)
+        mirror_use(copies, gradient)
         drain()
-        for c in range(band):
-            cols = slice(c * b, (c + 1) * b)
-            other = gm[0, c].T
-            gt[:, cols] = other
-            g = other.astype(jnp.float32) - gd[:, cols].astype(jnp.float32)
-            trow[:, cols] = (-STEP_SCALE * g).astype(trow.dtype)
-        spread_start(tflight, tw, trow)
-
+        spread_start(tflight)
+        spread_share(tflight, tw, trow)
         spread_finish(tw, -1, tflight)
         copies = mirror(1, xrow, tw, cf, gm.at[1])
-        mirror_wait(copies)
+        mirror_use(copies, commute)
         drain()
-        for c in range(band):
-            cols = slice(c * b, (c + 1) * b)
-            v = cf[:, cols].astype(jnp.float32) + gm[1, c].T.astype(jnp.float32)
-            ch[:, cols] = v.astype(ch.dtype)
-            base[:, cols] = dv[:, cols].astype(jnp.float32) + v
         product(ch, sw, co)
         copies = mirror(0, co, tw, qd, gm.at[2])
-        mirror_wait(copies)
-        for c in range(band):
-            qt[:, c * b:(c + 1) * b] = gm[2, c].T
+        mirror_use(copies, second)
 
     body()
     drain()

time: 48 us -> 46.8 us (0.975)
  Pallas kernels: 46.1 us -> 44.8 us
    pallas_call x1, Pallas kernels: 46.1 us -> 44.8 us  [local(): pl.pallas_call(functools.partial(kernel, ncol, n, b, half), out_shape=(ou...]
where the time goes in v3:
time: 46.8 us; the launch traced here: 46.6 us
  Pallas kernels  44.8 us (96%)
  other arithmetic  1.17 us (2%)
  between operations  0.64 us (1%)
    pallas_call x1, Pallas kernels, local(): pl.pallas_call(functools.partial(kernel, ncol, n, b, half), out_shape=(ou...  44.8 us
    add x1, other arithmetic, local(): return (gt - gd, base + 0.5 * (qd + qt))  1.17 us

profile of v3, /device:TPU:17, one launch (start us, length us, event | category | flops | bytes accessed | tf_op | source)
XLA Modules:
  0.0 46.6 jit_solution(6755506771876532052)
XLA Ops:
  0.6 44.8 %density_step.1 = (bf16[1,128,1152]{2,1,0:T(8,128)(2,1)S(1)}, bf16[1,128,1152]{2,1,0:T(8,128)(2,1)S(1)}, f32[1,128,1152]{2,1,0:T(8,128)S(1)}, bf16[1,128,1152]{2,1,0:T(8,128)(2,1)S(1)}, bf16[1,128,1152]{2,1,0:T(8,128)(2,1)S(1)}) custom-call(bf16[1,128,1152]{2,1,0:T(8,128)(2,1)} %margin.1, bf16[1,128,1152]{2,1,0:T(8,128)(2,1)} %fock.1, ...), custom_call_target="tpu_custom_call" | custom-call | tf_op jit(solution)/shard_map/density_step/pallas_call | solution.py:333
  45.5 1.2 %multiply_add_fusion = (f32[1,128,1152]{2,1,0:T(8,128)}, f32[1,128,1152]{2,1,0:T(8,128)}) fusion(f32[1,128,1152]{2,1,0:T(8,128)S(1)} %get-tuple-element.9, bf16[1,128,1152]{2,1,0:T(8,128)(2,1)S(1)} %get-tuple-element.11, bf16[1,128,1152]{2,1,0:T(8,128)(2,1)S(1)} %get-tuple-element.10, bf16[1,128,1152]{2,1,0:T(8,128)(2,1)S(1)} %get-tuple-element.8, ...), kind=kLoop, calls=%fused_computation | loop fusion | flops 1179648 | bytes 2949120 | tf_op jit(solution)/shard_map/add | solution.py:352

commit v4 on v3

--- a/solution.py
+++ b/solution.py
@@ -84,7 +84,6 @@
     offsets = [d for d in range(-half, half + 1) if d != 0]
     reach = half // 2
     hops = [e for m in range(reach, 0, -1) for e in (m, -m)]
-    send_order = sorted(hops, key=abs)
     received = [receive_plan(half, q) for q in (0, 1)]
     near = 2
     spots = len(hops) + near
@@ -169,12 +168,15 @@
                         moves.append((send, relay, e, q, cc, -e == 1 - 2 * q))
         return share, moves
 
-    def spread_start(flight):
+    def far_first(move):
+        return move[5], abs(move[2])
+
+    def spread_start(flight, key):
         for z in (0, 1):
             for cc in (0, 1):
                 @pl.when(both(parity == z, core == cc))
                 def _():
-                    for send, _, e, q, c, partner in sorted(flight[1], key=lambda m: send_order.index(m[2])):
+                    for send, _, e, q, c, partner in sorted(flight[1], key=key):
                         if (q + e) % 2 == z and c == cc:
                             if partner:
                                 send.start()
@@ -213,7 +215,7 @@
         flights.append(flight)
         reflect(w, sign, False)
 
-    def drain():
+    def drain(mirrored):
         for share, moves in flights:
             share.wait_send()
             for z in (0, 1):
@@ -232,9 +234,8 @@
                                 else:
                                     pl.when(valid_chip(-e))(relay.wait_send)
         flights.clear()
-        for cond, c in pending:
+        for cond, c in mirrored:
             pl.when(cond)(c.wait_send)
-        pending.clear()
 
     def mirror(phase, left, w, own, m):
         copies = []
@@ -291,35 +292,37 @@
         dflight, fflight = spread_plan(0, dv, dw), spread_plan(1, fv, fw)
         sflight, tflight = spread_plan(2, mv, sw), spread_plan(0, trow, tw)
         loads[0].wait()
-        spread_start(dflight)
+        spread_start(dflight, far_first)
         spread_share(dflight, dw, dv)
         loads[1].wait()
-        spread_start(fflight)
-        spread_share(fflight, fw, fv)
+        spread_start(fflight, far_first)
         loads[2].wait()
         loads[3].wait()
         spread_finish(dw, 1, dflight)
-        spread_start(sflight)
+        spread_share(fflight, fw, fv)
+        spread_start(sflight, far_first)
         spread_share(sflight, sw, mv)
         product(mv, dw, zrow)
         spread_finish(fw, 1, fflight)
         copies = mirror(0, zrow, fw, gd, gm.at[0])
         spread_finish(sw, 1, sflight)
         product(dv, sw, xrow)
+        drain([])
         mirror_use(copies, gradient)
-        drain()
-        spread_start(tflight)
+        spread_start(tflight, far_first)
         spread_share(tflight, tw, trow)
         spread_finish(tw, -1, tflight)
+        earlier = list(pending)
+        pending.clear()
         copies = mirror(1, xrow, tw, cf, gm.at[1])
+        drain(earlier)
         mirror_use(copies, commute)
-        drain()
         product(ch, sw, co)
         copies = mirror(0, co, tw, qd, gm.at[2])
         mirror_use(copies, second)
 
     body()
-    drain()
+    drain(pending)
 
 
 def local(ncol, n, margin, fock_matrix, density, present):

time: 46.8 us -> 46.2 us (0.987)
  Pallas kernels: 44.8 us -> 44.3 us
    pallas_call x1, Pallas kernels: 44.8 us -> 44.3 us  [local(): pl.pallas_call(functools.partial(kernel, ncol, n, b, half), out_shape=(ou...]
where the time goes in v4:
time: 46.2 us; the launch traced here: 46.1 us
  Pallas kernels  44.3 us (96%)
  other arithmetic  1.17 us (3%)
  between operations  0.64 us (1%)
    pallas_call x1, Pallas kernels, local(): pl.pallas_call(functools.partial(kernel, ncol, n, b, half), out_shape=(ou...  44.3 us
    add x1, other arithmetic, local(): return (gt - gd, base + 0.5 * (qd + qt))  1.17 us

profile of v4, /device:TPU:17, one launch (start us, length us, event | category | flops | bytes accessed | tf_op | source)
XLA Modules:
  0.0 46.1 jit_solution(10952235576436144960)
XLA Ops:
  0.6 44.3 %density_step.1 = (bf16[1,128,1152]{2,1,0:T(8,128)(2,1)S(1)}, bf16[1,128,1152]{2,1,0:T(8,128)(2,1)S(1)}, f32[1,128,1152]{2,1,0:T(8,128)S(1)}, bf16[1,128,1152]{2,1,0:T(8,128)(2,1)S(1)}, bf16[1,128,1152]{2,1,0:T(8,128)(2,1)S(1)}) custom-call(bf16[1,128,1152]{2,1,0:T(8,128)(2,1)} %margin.1, bf16[1,128,1152]{2,1,0:T(8,128)(2,1)} %fock.1, ...), custom_call_target="tpu_custom_call" | custom-call | tf_op jit(solution)/shard_map/density_step/pallas_call | solution.py:336
  44.9 1.2 %multiply_add_fusion = (f32[1,128,1152]{2,1,0:T(8,128)}, f32[1,128,1152]{2,1,0:T(8,128)}) fusion(f32[1,128,1152]{2,1,0:T(8,128)S(1)} %get-tuple-element.9, bf16[1,128,1152]{2,1,0:T(8,128)(2,1)S(1)} %get-tuple-element.11, bf16[1,128,1152]{2,1,0:T(8,128)(2,1)S(1)} %get-tuple-element.10, bf16[1,128,1152]{2,1,0:T(8,128)(2,1)S(1)} %get-tuple-element.8, ...), kind=kLoop, calls=%fused_computation | loop fusion | flops 1179648 | bytes 2949120 | tf_op jit(solution)/shard_map/add | solution.py:355

commit v5 on v4

--- a/solution.py
+++ b/solution.py
@@ -319,10 +319,10 @@
         mirror_use(copies, commute)
         product(ch, sw, co)
         copies = mirror(0, co, tw, qd, gm.at[2])
+        drain(pending)
         mirror_use(copies, second)
 
     body()
-    drain(pending)
 
 
 def local(ncol, n, margin, fock_matrix, density, present):

time: 46.2 us -> 46.2 us (level)
  no operation moved by 1% of the time
where the time goes in v5:
time: 46.2 us; the launch traced here: 46.1 us
  Pallas kernels  44.3 us (96%)
  other arithmetic  1.17 us (3%)
  between operations  0.64 us (1%)
    pallas_call x1, Pallas kernels, local(): pl.pallas_call(functools.partial(kernel, ncol, n, b, half), out_shape=(ou...  44.3 us
    add x1, other arithmetic, local(): return (gt - gd, base + 0.5 * (qd + qt))  1.17 us

profile of v5, /device:TPU:17, one launch (start us, length us, event | category | flops | bytes accessed | tf_op | source)
XLA Modules:
  0.0 46.1 jit_solution(7151114088696025833)
XLA Ops:
  0.6 44.3 %density_step.1 = (bf16[1,128,1152]{2,1,0:T(8,128)(2,1)S(1)}, bf16[1,128,1152]{2,1,0:T(8,128)(2,1)S(1)}, f32[1,128,1152]{2,1,0:T(8,128)S(1)}, bf16[1,128,1152]{2,1,0:T(8,128)(2,1)S(1)}, bf16[1,128,1152]{2,1,0:T(8,128)(2,1)S(1)}) custom-call(bf16[1,128,1152]{2,1,0:T(8,128)(2,1)} %margin.1, bf16[1,128,1152]{2,1,0:T(8,128)(2,1)} %fock.1, ...), custom_call_target="tpu_custom_call" | custom-call | tf_op jit(solution)/shard_map/density_step/pallas_call | solution.py:336
  44.9 1.2 %multiply_add_fusion = (f32[1,128,1152]{2,1,0:T(8,128)}, f32[1,128,1152]{2,1,0:T(8,128)}) fusion(f32[1,128,1152]{2,1,0:T(8,128)S(1)} %get-tuple-element.9, bf16[1,128,1152]{2,1,0:T(8,128)(2,1)S(1)} %get-tuple-element.11, bf16[1,128,1152]{2,1,0:T(8,128)(2,1)S(1)} %get-tuple-element.10, bf16[1,128,1152]{2,1,0:T(8,128)(2,1)S(1)} %get-tuple-element.8, ...), kind=kLoop, calls=%fused_computation | loop fusion | flops 1179648 | bytes 2949120 | tf_op jit(solution)/shard_map/add | solution.py:355
